TPU v7x, 32 devices: a whole 2x2x4 slice. The times are simulated.
32 devices in a mesh: group: 8 (over z, y), lat: 2 (over x), rad: 2 (over core).
Axes of the slice: x: 2, y: 2, z: 4, core: 2. Of those that a mesh axis runs over, the one named last changes fastest.
Arguments:
- displacement_prev: float32 [3, 4, 128, 256], P(None, 'rad', 'group', 'lat'), may hold values from -2.5 to 2.5
- shear_modulus: float32 [4, 128, 256], P('rad', 'group', 'lat'), may hold values from 1 to 10
- viscosity: float32 [4, 128, 256], P('rad', 'group', 'lat'), may hold values from 0.5 to 20
- element_matrix: float32 [24, 24], replicated, as said below
- regrid_index: int32 [128, 2, 4], P('group', 'lat'), may hold values from 0 to 63
- regrid_weight: float32 [128, 2, 4], P('group', 'lat'), may hold values from 0.1 to 0.6
- ice_thickness: float32 [32, 256], P('lat'), may hold values from 0.5 to 4
- bed_elevation: float32 [32, 256], P('lat'), may hold values from -3 to 3
- basal_friction: float32 [32, 256], P('lat'), may hold values from 0.2 to 5
- ice_mask: int32 [32, 256], P('lat'), may hold values 0 or 1
- speed_guess: float32 [16, 32, 256], P(None, 'lat'), may hold values from -3 to 3
Outputs:
- displacement: float32 [3, 4, 128, 256], P(None, 'rad', 'group', 'lat')
- bed_new: float32 [32, 256], P('lat')
Inputs may be any that keep to these rules, and one draw needn't show every extreme that they name: `regrid_index`: names a block of the ice map: block b is row b // 2, columns 128 * (b % 2) to 128 * (b % 2) + 127. `element_matrix`: symmetric positive definite.
All inputs are finite; a program needn't handle non-finite values. No bound on the sum of `ice_mask` on one device may be relied on, other than what follows from the above.
Results may differ from a plain program's by a relative error of at most 0.0019.
Values may be sent and summed in bfloat16 or wider, within the bound.
No kernel may reach another device: no remote copies, remote signals or barrier semaphores. Data moves between devices by JAX's collectives and lax.ppermute only.
A program may use at most 64 MiB of HBM per device.

v0:
```python
import jax
import jax.numpy as jnp
from jax import lax
from jax.sharding import PartitionSpec as P

BLOCK = 128
SWEEPS = 6
ITERS = 4
LOAD_SCALE = 20.0
UPLIFT_SCALE = 0.5
TIME_SCALE = 1.0
ICE_STEP = 0.5
ASPECT = 0.01
STRAIN_FLOOR = 0.01
CORNERS = [
    (layer_bit, row_bit, col_bit)
    for layer_bit in (0, 1)
    for row_bit in (0, 1)
    for col_bit in (0, 1)
]


def padded(cells, sides, width):
    for axis, dim in sides:
        count = lax.axis_size(axis)
        ends = count - 1
        head = lax.slice_in_dim(cells, 0, width, axis=dim)
        tail = lax.slice_in_dim(cells, cells.shape[dim] - width, cells.shape[dim], axis=dim)
        cells = jnp.concatenate(
            [
                lax.ppermute(tail, axis, [(i, (i + 1) % count) for i in range(ends)]),
                cells,
                lax.ppermute(head, axis, [((i + 1) % count, i) for i in range(ends)]),
            ],
            axis=dim,
        )
    return cells


def broadcast(value, axis, source):
    kept = jnp.where(lax.axis_index(axis) == source, value, 0).astype(value.dtype)
    return lax.psum(kept, axis)


def corner_mean(padded_coef):
    layer_count = padded_coef.shape[0] - 1
    col_count = padded_coef.shape[1] - 1
    depth_count = padded_coef.shape[2] - 1
    summed = jnp.zeros((layer_count, col_count, depth_count), jnp.float32)
    for layer_bit, row_bit, col_bit in CORNERS:
        summed = (
            summed
            + padded_coef[
                layer_bit : layer_bit + layer_count,
                row_bit : row_bit + col_count,
                col_bit : col_bit + depth_count,
            ]
        )
    return summed / 8.0


def element_apply(padded_field, element_coef, kernel):
    layer_count, col_count, depth_count = element_coef.shape
    pieces = [
        padded_field[
            :,
            layer_bit : layer_bit + layer_count,
            row_bit : row_bit + col_count,
            col_bit : col_bit + depth_count,
        ]
        for layer_bit, row_bit, col_bit in CORNERS
    ]
    stacked = jnp.concatenate(pieces, 0)
    forces = (
        jnp.einsum("pq,qrab->prab", kernel, stacked, precision=lax.Precision.HIGHEST) * element_coef
    )
    summed = jnp.zeros((3, layer_count - 1, col_count - 1, depth_count - 1), jnp.float32)
    for corner_id, (layer_bit, row_bit, col_bit) in enumerate(CORNERS):
        summed = (
            summed
            + forces[
                3 * corner_id : 3 * corner_id + 3,
                1 - layer_bit : layer_count - layer_bit,
                1 - row_bit : col_count - row_bit,
                1 - col_bit : depth_count - col_bit,
            ]
        )
    return summed


def column_neighbours(values):
    zero_col = jnp.zeros_like(values[..., :1])
    east_side = jnp.concatenate([values[..., 1:], zero_col], -1)
    west_side = jnp.concatenate([zero_col, values[..., :-1]], -1)
    return (east_side, west_side)


def ice_sweep(velocity, padded_speed, thickness, friction, driving):
    levels = velocity.shape[0]
    north_side = padded_speed[:, 2:, :]
    south_side = padded_speed[:, :-2, :]
    east_side, west_side = column_neighbours(velocity)
    inverse = (levels - 1) / thickness
    slope_rows = 0.5 * (north_side - south_side)
    slope_cols = 0.5 * (east_side - west_side)
    slope_levels = (
        jnp.concatenate(
            [
                velocity[1:2] - velocity[0:1],
                0.5 * (velocity[2:] - velocity[:-2]),
                velocity[-1:] - velocity[-2:-1],
            ],
            0,
        )
        * inverse
    )
    strain = slope_rows**2 + 0.25 * slope_cols**2 + 0.25 * slope_levels**2 + STRAIN_FLOOR
    stiffness = 0.5 * strain ** (-1.0 / 3.0)
    vertical = ASPECT * inverse**2 * 0.5 * (stiffness[1:] + stiffness[:-1])
    neighbours = stiffness * (north_side + south_side + east_side + west_side)
    factors = []
    upper_prev = None
    values_prev = None
    for level_id in range(levels):
        diagonal = 4.0 * stiffness[level_id]
        if level_id > 0:
            diagonal = diagonal + vertical[level_id - 1]
        if level_id < levels - 1:
            diagonal = diagonal + vertical[level_id]
        if level_id == 0:
            diagonal = diagonal + friction
        right_side = driving + neighbours[level_id]
        if level_id > 0:
            lower_coef = -vertical[level_id - 1]
            diagonal = diagonal - lower_coef * upper_prev
            right_side = right_side - lower_coef * values_prev
        upper_prev = -vertical[level_id] / diagonal if level_id < levels - 1 else None
        values_prev = right_side / diagonal
        factors.append((upper_prev, values_prev))
    solution = [None] * levels
    solution[levels - 1] = factors[levels - 1][1]
    for level_id in range(levels - 2, -1, -1):
        solution[level_id] = factors[level_id][1] - factors[level_id][0] * solution[level_id + 1]
    return jnp.stack(solution, 0)


def ice_tile_load(is_ice, ice_thickness, bed_elevation, basal_friction, ice_mask, speed_guess):
    ice_present = ice_mask.astype(jnp.float32)
    surface = bed_elevation + ice_thickness
    padded_surface = padded(surface, (("lat", 0),), 1)
    driving = -ice_present * ice_thickness * 0.5 * (padded_surface[2:] - padded_surface[:-2])
    velocity = speed_guess
    for sweep_id in range(SWEEPS):
        padded_speed = padded(velocity, (("lat", 1),), 1)

        def run_sweep(operands):
            return ice_sweep(operands[0], operands[1], ice_thickness, basal_friction, driving)

        def keep_speed(operands):
            return operands[0]

        velocity = lax.cond(is_ice, run_sweep, keep_speed, (velocity, padded_speed))
    ice_flux = ice_thickness * jnp.mean(velocity, 0)
    padded_flux = padded(ice_flux, (("lat", 0),), 1)
    new_thickness = ice_thickness - ICE_STEP * 0.5 * (padded_flux[2:] - padded_flux[:-2])
    ice_load = (ice_present * new_thickness).astype(jnp.bfloat16)
    return jnp.where(is_ice, ice_load, jnp.zeros_like(ice_load))


def per_device(
    displacement_prev,
    shear_modulus,
    viscosity,
    element_matrix,
    regrid_index,
    regrid_weight,
    ice_thickness,
    bed_elevation,
    basal_friction,
    ice_mask,
    speed_guess,
):
    ice_root = lax.axis_size("group") - 1
    is_ice = lax.axis_index("group") == ice_root
    shell_group = (lax.axis_index("group") < ice_root).astype(jnp.float32)
    top_core = (lax.axis_index("rad") == 0).astype(jnp.float32)
    relax_ratio = TIME_SCALE * shear_modulus / viscosity
    modulus = shell_group * shear_modulus / (1.0 + relax_ratio)
    relaxed = modulus * relax_ratio / (1.0 + relax_ratio)
    start_field = displacement_prev * shell_group
    joined = jnp.concatenate([start_field, modulus[None], relaxed[None]], 0)
    padded_all = padded(joined, (("group", 2), ("lat", 3), ("rad", 1)), 1)
    coef_main = corner_mean(padded_all[3])
    coef_relax = corner_mean(padded_all[4])
    ice_load = ice_tile_load(
        is_ice, ice_thickness, bed_elevation, basal_friction, ice_mask, speed_guess
    )

    def skip_shell(unused):
        return jnp.zeros(start_field.shape, jnp.float32)

    def shell_branch(unused):
        return element_apply(padded_all[:3], coef_relax, element_matrix) * shell_group

    relax_force = lax.cond(is_ice, skip_shell, shell_branch, 0)
    shell_tile = broadcast(ice_load, "group", ice_root)
    ice_field = lax.all_gather(shell_tile, "lat", axis=0, tiled=True)
    row_count = regrid_index.shape[0]
    flat_index = regrid_index.reshape(-1)
    weights = regrid_weight.reshape(row_count, -1)
    blocks = ice_field.reshape(-1, BLOCK)
    picked = jnp.take(blocks, flat_index, axis=0).astype(jnp.float32).reshape(row_count, -1, BLOCK)
    surface_thickness = jnp.sum(weights[..., None] * picked, 1)
    load_field = (
        jnp.zeros(start_field.shape, jnp.float32)
        .at[2, 0]
        .set(-LOAD_SCALE * surface_thickness * top_core * shell_group)
    )
    residual = load_field - relax_force

    def global_norm(values):
        return lax.psum(jnp.sum(values * values), ("group", "lat", "rad"))

    solution = start_field
    direction = residual
    norm_now = global_norm(residual)
    for iter_id in range(ITERS):
        padded_field = padded(direction, (("group", 2), ("lat", 3), ("rad", 1)), 1)
        mapped = element_apply(padded_field, coef_main, element_matrix) * shell_group
        step_size = norm_now / lax.psum(jnp.sum(direction * mapped), ("group", "lat", "rad"))
        solution = solution + step_size * direction
        residual = residual - step_size * mapped
        norm_next = global_norm(residual)
        direction = residual + norm_next / norm_now * direction
        norm_now = norm_next
    layer_total = solution.shape[1] * lax.axis_size("rad")
    surface_lift = jnp.sum(solution[2], 0) / layer_total
    contrib = (weights[..., None] * surface_lift[:, None, :]).reshape(-1, BLOCK)
    tile_height = 2 * ice_thickness.shape[0]
    targets = lax.broadcasted_iota(
        jnp.int32, (tile_height * lax.axis_size("lat"), flat_index.shape[0]), 0
    )
    selector = (targets == flat_index[None, :]).astype(jnp.float32)
    all_lift = lax.psum(
        jnp.dot(
            selector, contrib, precision=lax.Precision.HIGHEST, preferred_element_type=jnp.float32
        ),
        ("group", "lat", "rad"),
    )
    own_lift = lax.dynamic_slice_in_dim(
        all_lift, lax.axis_index("lat") * tile_height, tile_height, 0
    )
    bed_new = bed_elevation + UPLIFT_SCALE * own_lift.reshape(bed_elevation.shape)
    return (solution, bed_new)


def solution(mesh):
    in_specs = (
        P(None, "rad", "group", "lat"),
        P("rad", "group", "lat"),
        P("rad", "group", "lat"),
        P(),
        P("group", "lat", None),
        P("group", "lat", None),
        P("lat", None),
        P("lat", None),
        P("lat", None),
        P("lat", None),
        P(None, "lat", None),
    )
    out_specs = (P(None, "rad", "group", "lat"), P("lat", None))
    return jax.shard_map(
        per_device, mesh=mesh, in_specs=in_specs, out_specs=out_specs, check_vma=False
    )
```

profile of v0, /device:TPU:0, one launch (start us, length us, event | category | flops | bytes accessed | tf_op | source)
XLA Modules:
  0.0 650.5 jit_solution(13611516230514924410)
XLA Ops:
  5.3 5.5 collective-permute-start.16
  13.8 4.5 collective-permute-start.3
  21.3 4.5 collective-permute-start
  30.6 4.5 collective-permute-start.4
  40.4 4.5 collective-permute-start.6
  49.7 4.5 collective-permute-start.8
  55.7 4.6 collective-permute-start.18
  63.6 4.5 collective-permute-start.10
  72.9 4.5 collective-permute-start.12
  89.9 7.3 %conditional.13 = (f32[3,2,16,128]{3,0,2,1:T(4,128)S(1)}) conditional(s32[]{:T(128)} %convert_element_type.28, (f32[5,4,18,130]{3,0,2,1:T(8,128)S(1)}, f32[24,24]{1,0:T(8,128)S(1)}, f32[3,17,129]{2,0,1:T(4,128)}, f32[]{:T(128)}) %tuple.375, () %tuple.72), branch_computations={%region_15.16_spmd, %region_16.17_spmd} | conditional | flops 45782880 | bytes 5078236 | solution.py:205
  90.4 4.3 concatenate.158
  98.1 87.5 %psum.70 = bf16[16,256]{1,0:T(8,128)(2,1)S(1)} all-reduce(bf16[16,256]{1,0:T(8,128)(2,1)S(1)} %select_select_fusion), channel_id=1, replica_groups=mesh['group'=8,'lat'=2,'rad'=2] {'group'}, use_global_device_ids=true, to_apply=%region_13.14 | all-reduce | flops 4096 | bytes 16384 | tf_op jit(solution)/shard_map/psum | solution.py:42
  185.6 4.4 all_gather.3
  192.9 4.5 collective-permute-start.22
  200.2 4.5 collective-permute-start.24
  213.0 4.3 concatenate.211
  219.4 40.3 %all-reduce.13 = (f32[]{:T(128)}, f32[]{:T(128)}) all-reduce(f32[]{:T(128)} %get-tuple-element.190, f32[]{:T(128)} %get-tuple-element.189), channel_id=1, replica_groups=mesh['group'=8,'lat'=2,'rad'=2] {'group','lat','rad'}, use_global_device_ids=true, to_apply=%region_18.19 | all-reduce | flops 2 | bytes 16 | tf_op jit(solution)/shard_map/psum | solution.py:222
  261.7 40.9 %psum.73 = f32[]{:T(128)} all-reduce(f32[]{:T(128)} %multiply_reduce_fusion.4), channel_id=1, replica_groups=mesh['group'=8,'lat'=2,'rad'=2] {'group','lat','rad'}, use_global_device_ids=true, to_apply=%region_22.23 | all-reduce | flops 1 | bytes 8 | tf_op jit(solution)/shard_map/psum | solution.py:222
  305.2 5.0 collective-permute-start.28
  313.0 4.5 collective-permute-start.30
  325.8 4.3 concatenate.216
  332.2 43.2 %psum.74 = f32[]{:T(128)} all-reduce(f32[]{:T(128)} %get-tuple-element.399), channel_id=1, replica_groups=mesh['group'=8,'lat'=2,'rad'=2] {'group','lat','rad'}, use_global_device_ids=true, to_apply=%region_24.25 | all-reduce | flops 1 | bytes 8 | tf_op jit(solution)/shard_map/psum | solution.py:230
  377.3 40.4 %psum.75 = f32[]{:T(128)} all-reduce(f32[]{:T(128)} %get-tuple-element.397), channel_id=1, replica_groups=mesh['group'=8,'lat'=2,'rad'=2] {'group','lat','rad'}, use_global_device_ids=true, to_apply=%region_26.27 | all-reduce | flops 1 | bytes 8 | tf_op jit(solution)/shard_map/psum | solution.py:222
  420.4 5.0 collective-permute-start.34
  428.1 4.5 collective-permute-start.36
  441.0 4.3 concatenate.221
  447.3 43.4 %psum.76 = f32[]{:T(128)} all-reduce(f32[]{:T(128)} %get-tuple-element.395), channel_id=1, replica_groups=mesh['group'=8,'lat'=2,'rad'=2] {'group','lat','rad'}, use_global_device_ids=true, to_apply=%region_28.29 | all-reduce | flops 1 | bytes 8 | tf_op jit(solution)/shard_map/psum | solution.py:230
  492.7 41.1 %psum.77 = f32[]{:T(128)} all-reduce(f32[]{:T(128)} %multiply_reduce_fusion), channel_id=1, replica_groups=mesh['group'=8,'lat'=2,'rad'=2] {'group','lat','rad'}, use_global_device_ids=true, to_apply=%region_30.31 | all-reduce | flops 1 | bytes 8 | tf_op jit(solution)/shard_map/psum | solution.py:222
  536.5 5.0 collective-permute-start.40
  544.3 4.5 collective-permute-start.42
  563.5 43.2 %psum.78 = f32[]{:T(128)} all-reduce(f32[]{:T(128)} %fusion.707), channel_id=1, replica_groups=mesh['group'=8,'lat'=2,'rad'=2] {'group','lat','rad'}, use_global_device_ids=true, to_apply=%region_32.33 | all-reduce | flops 1 | bytes 8 | tf_op jit(solution)/shard_map/psum | solution.py:230
  609.0 40.8 %psum.79 = f32[64,128]{1,0:T(8,128)S(1)} all-reduce(f32[64,128]{1,0:T(8,128)S(1)} %fusion.711), channel_id=1, replica_groups=mesh['group'=8,'lat'=2,'rad'=2] {'group','lat','rad'}, use_global_device_ids=true, to_apply=%region_34.35 | all-reduce | flops 8192 | bytes 65536 | tf_op jit(solution)/shard_map/psum | solution.py:244
  (204 shorter events, 118.1 us)
Async XLA Ops:
  4.0 41.0 %collective-permute-start.17 = (f32[5,2,1,128]{3,0,2,1:T(8,128)S(1)}, f32[5,2,1,128]{3,0,2,1:T(8,128)S(1)}, u32[]{:S(2)}, u32[]{:S(2)}) collective-permute-start(f32[5,2,1,128]{3,0,2,1:T(8,128)S(1)} %get-tuple-element.513), channel_id=1, source_target_pairs={{4,0},{8,4},{12,8},{16,12},{20,16},{24,20},{28,24},{5,1},{9,5},{13... | collective-permute-start | bytes 15368 | tf_op jit(solution)/shard_map/ppermute | solution.py:33
  5.3 39.7 %collective-permute-start.16 = (f32[5,2,1,128]{3,0,2,1:T(8,128)S(1)}, f32[5,2,1,128]{3,0,2,1:T(8,128)S(1)}, u32[]{:S(2)}, u32[]{:S(2)}) collective-permute-start(f32[5,2,1,128]{3,0,2,1:T(8,128)S(1)} %get-tuple-element.512), channel_id=1, source_target_pairs={{0,4},{4,8},{8,12},{12,16},{16,20},{20,24},{24,28},{1,5},{5,9},{9,... | collective-permute-start | bytes 15368 | tf_op jit(solution)/shard_map/ppermute | solution.py:31
  11.8 14.8 %collective-permute-start.1 = (f32[16,1,256]{2,1,0:T(1,128)S(1)}, f32[16,1,256]{2,1,0:T(1,128)S(1)}, u32[]{:S(2)}, u32[]{:S(2)}) collective-permute-start(f32[16,1,256]{2,1,0:T(1,128)S(1)} %get-tuple-element.461), channel_id=1, source_target_pairs={{2,0},{3,1},{6,4},{7,5},{10,8},{11,9},{14,12},{15,13},{18,16},{19,... | collective-permute-start | bytes 49160 | tf_op jit(solution)/shard_map/ppermute | solution.py:33
  13.8 7.4 %collective-permute-start.3 = (f32[1,256]{1,0:T(1,128)S(1)}, f32[1,256]{1,0:T(1,128)S(1)}, u32[]{:S(2)}, u32[]{:S(2)}) collective-permute-start(f32[1,256]{1,0:T(1,128)S(1)} %get-tuple-element.533), channel_id=1, source_target_pairs={{0,2},{1,3},{4,6},{5,7},{8,10},{9,11},{12,14},{13,15},{16,18},{17,... | collective-permute-start | bytes 3080 | tf_op jit(solution)/shard_map/ppermute | solution.py:31
  18.4 7.4 %collective-permute-start.2 = (f32[1,256]{1,0:T(1,128)S(1)}, f32[1,256]{1,0:T(1,128)S(1)}, u32[]{:S(2)}, u32[]{:S(2)}) collective-permute-start(f32[1,256]{1,0:T(1,128)S(1)} %get-tuple-element.532), channel_id=1, source_target_pairs={{2,0},{3,1},{6,4},{7,5},{10,8},{11,9},{14,12},{15,13},{18,16},{19,... | collective-permute-start | bytes 3080 | tf_op jit(solution)/shard_map/ppermute | solution.py:33
  29.3 7.8 %collective-permute-start.5 = (f32[16,1,256]{2,1,0:T(1,128)S(1)}, f32[16,1,256]{2,1,0:T(1,128)S(1)}, u32[]{:S(2)}, u32[]{:S(2)}) collective-permute-start(f32[16,1,256]{2,1,0:T(1,128)S(1)} %get-tuple-element.459), channel_id=1, source_target_pairs={{2,0},{3,1},{6,4},{7,5},{10,8},{11,9},{14,12},{15,13},{18,16},{19,... | collective-permute-start | bytes 49160 | tf_op jit(solution)/shard_map/ppermute | solution.py:33
  30.6 6.5 %collective-permute-start.4 = (f32[16,1,256]{2,1,0:T(1,128)S(1)}, f32[16,1,256]{2,1,0:T(1,128)S(1)}, u32[]{:S(2)}, u32[]{:S(2)}) collective-permute-start(f32[16,1,256]{2,1,0:T(1,128)S(1)} %get-tuple-element.458), channel_id=1, source_target_pairs={{0,2},{1,3},{4,6},{5,7},{8,10},{9,11},{12,14},{13,15},{16,18},{17,... | collective-permute-start | bytes 49160 | tf_op jit(solution)/shard_map/ppermute | solution.py:31
  48.4 11.8 %collective-permute-start.9 = (f32[16,1,256]{2,1,0:T(1,128)S(1)}, f32[16,1,256]{2,1,0:T(1,128)S(1)}, u32[]{:S(2)}, u32[]{:S(2)}) collective-permute-start(f32[16,1,256]{2,1,0:T(1,128)S(1)} %get-tuple-element.455), channel_id=1, source_target_pairs={{2,0},{3,1},{6,4},{7,5},{10,8},{11,9},{14,12},{15,13},{18,16},{19,... | collective-permute-start | bytes 49160 | tf_op jit(solution)/shard_map/ppermute | solution.py:33
  49.7 10.5 %collective-permute-start.8 = (f32[16,1,256]{2,1,0:T(1,128)S(1)}, f32[16,1,256]{2,1,0:T(1,128)S(1)}, u32[]{:S(2)}, u32[]{:S(2)}) collective-permute-start(f32[16,1,256]{2,1,0:T(1,128)S(1)} %get-tuple-element.454), channel_id=1, source_target_pairs={{0,2},{1,3},{4,6},{5,7},{8,10},{9,11},{12,14},{13,15},{16,18},{17,... | collective-permute-start | bytes 49160 | tf_op jit(solution)/shard_map/ppermute | solution.py:31
  54.4 13.8 %collective-permute-start.19 = (f32[5,2,18,1]{3,0,2,1:T(8,128)S(1)}, f32[5,2,18,1]{3,0,2,1:T(8,128)S(1)}, u32[]{:S(2)}, u32[]{:S(2)}) collective-permute-start(f32[5,2,18,1]{3,0,2,1:T(8,128)S(1)} %get-tuple-element.511), channel_id=1, source_target_pairs={{2,0},{3,1},{6,4},{7,5},{10,8},{11,9},{14,12},{15,13},{18,16},{19,... | collective-permute-start | bytes 2168 | tf_op jit(solution)/shard_map/ppermute | solution.py:33
  55.7 12.5 %collective-permute-start.18 = (f32[5,2,18,1]{3,0,2,1:T(8,128)S(1)}, f32[5,2,18,1]{3,0,2,1:T(8,128)S(1)}, u32[]{:S(2)}, u32[]{:S(2)}) collective-permute-start(f32[5,2,18,1]{3,0,2,1:T(8,128)S(1)} %get-tuple-element.510), channel_id=1, source_target_pairs={{0,2},{1,3},{4,6},{5,7},{8,10},{9,11},{12,14},{13,15},{16,18},{17,... | collective-permute-start | bytes 2168 | tf_op jit(solution)/shard_map/ppermute | solution.py:31
  62.3 6.2 collective-permute-start.11
  71.6 10.2 %collective-permute-start.13 = (f32[16,1,256]{2,1,0:T(1,128)S(1)}, f32[16,1,256]{2,1,0:T(1,128)S(1)}, u32[]{:S(2)}, u32[]{:S(2)}) collective-permute-start(f32[16,1,256]{2,1,0:T(1,128)S(1)} %get-tuple-element.451), channel_id=1, source_target_pairs={{2,0},{3,1},{6,4},{7,5},{10,8},{11,9},{14,12},{15,13},{18,16},{19,... | collective-permute-start | bytes 49160 | tf_op jit(solution)/shard_map/ppermute | solution.py:33
  72.9 8.9 %collective-permute-start.12 = (f32[16,1,256]{2,1,0:T(1,128)S(1)}, f32[16,1,256]{2,1,0:T(1,128)S(1)}, u32[]{:S(2)}, u32[]{:S(2)}) collective-permute-start(f32[16,1,256]{2,1,0:T(1,128)S(1)} %get-tuple-element.450), channel_id=1, source_target_pairs={{0,2},{1,3},{4,6},{5,7},{8,10},{9,11},{12,14},{13,15},{16,18},{17,... | collective-permute-start | bytes 49160 | tf_op jit(solution)/shard_map/ppermute | solution.py:31
  77.5 11.5 %collective-permute-start.21 = (f32[5,1,18,130]{3,0,2,1:T(8,128)S(1)}, f32[5,1,18,130]{3,0,2,1:T(8,128)S(1)}, u32[]{:S(2)}, u32[]{:S(2)}) collective-permute-start(f32[5,1,18,130]{3,0,2,1:T(8,128)S(1)} %get-tuple-element.449), channel_id=1, source_target_pairs={{1,0},{3,2},{5,4},{7,6},{9,8},{11,10},{13,12},{15,14},{17,16},{19,... | collective-permute-start | bytes 140408 | tf_op jit(solution)/shard_map/ppermute | solution.py:33
  78.8 10.2 %collective-permute-start.20 = (f32[5,1,18,130]{3,0,2,1:T(8,128)S(1)}, f32[5,1,18,130]{3,0,2,1:T(8,128)S(1)}, u32[]{:S(2)}, u32[]{:S(2)}) collective-permute-start(f32[5,1,18,130]{3,0,2,1:T(8,128)S(1)} %get-tuple-element.448), channel_id=1, source_target_pairs={{0,1},{2,3},{4,5},{6,7},{8,9},{10,11},{12,13},{14,15},{16,17},{18,... | collective-permute-start | bytes 140408 | tf_op jit(solution)/shard_map/ppermute | solution.py:31
  85.8 11.4 %collective-permute-start.15 = (f32[1,256]{1,0:T(1,128)}, f32[1,256]{1,0:T(1,128)}, u32[]{:S(2)}, u32[]{:S(2)}) collective-permute-start(f32[1,256]{1,0:T(1,128)} %get-tuple-element.531), channel_id=1, source_target_pairs={{0,2},{1,3},{4,6},{5,7},{8,10},{9,11},{12,14},{13,15},{16,18},{17,... | collective-permute-start | bytes 3080 | tf_op jit(solution)/shard_map/ppermute | solution.py:31
  87.6 9.6 %collective-permute-start.14 = (f32[1,256]{1,0:T(1,128)}, f32[1,256]{1,0:T(1,128)}, u32[]{:S(2)}, u32[]{:S(2)}) collective-permute-start(f32[1,256]{1,0:T(1,128)} %get-tuple-element.530), channel_id=1, source_target_pairs={{2,0},{3,1},{6,4},{7,5},{10,8},{11,9},{14,12},{15,13},{18,16},{19,... | collective-permute-start | bytes 3080 | tf_op jit(solution)/shard_map/ppermute | solution.py:33
  198.9 6.2 collective-permute-start.25
  200.2 6.5 %collective-permute-start.24 = (f32[3,2,18,1]{3,0,2,1:T(4,128)S(1)}, f32[3,2,18,1]{3,0,2,1:T(4,128)S(1)}, u32[]{:S(2)}, u32[]{:S(2)}) collective-permute-start(f32[3,2,18,1]{3,0,2,1:T(4,128)S(1)} %get-tuple-element.520), channel_id=1, source_target_pairs={{0,2},{1,3},{4,6},{5,7},{8,10},{9,11},{12,14},{13,15},{16,18},{17,... | collective-permute-start | bytes 1304 | tf_op jit(solution)/shard_map/ppermute | solution.py:31
  303.9 6.3 collective-permute-start.29
  305.2 6.3 collective-permute-start.28
  311.7 6.2 collective-permute-start.31
  313.0 6.5 %collective-permute-start.30 = (f32[3,2,18,1]{3,0,2,1:T(4,128)S(1)}, f32[3,2,18,1]{3,0,2,1:T(4,128)S(1)}, u32[]{:S(2)}, u32[]{:S(2)}) collective-permute-start(f32[3,2,18,1]{3,0,2,1:T(4,128)S(1)} %get-tuple-element.518), channel_id=1, source_target_pairs={{0,2},{1,3},{4,6},{5,7},{8,10},{9,11},{12,14},{13,15},{16,18},{17,... | collective-permute-start | bytes 1304 | tf_op jit(solution)/shard_map/ppermute | solution.py:31
  419.1 6.3 collective-permute-start.35
  420.4 6.3 collective-permute-start.34
  426.8 6.2 collective-permute-start.37
  428.1 6.5 %collective-permute-start.36 = (f32[3,2,18,1]{3,0,2,1:T(4,128)S(1)}, f32[3,2,18,1]{3,0,2,1:T(4,128)S(1)}, u32[]{:S(2)}, u32[]{:S(2)}) collective-permute-start(f32[3,2,18,1]{3,0,2,1:T(4,128)S(1)} %get-tuple-element.516), channel_id=1, source_target_pairs={{0,2},{1,3},{4,6},{5,7},{8,10},{9,11},{12,14},{13,15},{16,18},{17,... | collective-permute-start | bytes 1304 | tf_op jit(solution)/shard_map/ppermute | solution.py:31
  535.2 6.3 collective-permute-start.41
  536.5 6.3 collective-permute-start.40
  543.0 6.2 collective-permute-start.43
  544.3 6.5 %collective-permute-start.42 = (f32[3,2,18,1]{3,0,2,1:T(4,128)S(1)}, f32[3,2,18,1]{3,0,2,1:T(4,128)S(1)}, u32[]{:S(2)}, u32[]{:S(2)}) collective-permute-start(f32[3,2,18,1]{3,0,2,1:T(4,128)S(1)} %get-tuple-element.514), channel_id=1, source_target_pairs={{0,2},{1,3},{4,6},{5,7},{8,10},{9,11},{12,14},{13,15},{16,18},{17,... | collective-permute-start | bytes 1304 | tf_op jit(solution)/shard_map/ppermute | solution.py:31
  (21 other events, 273.1 us)
where the time goes:
time: 655 us; the launch traced here: 650 us
  blocking collectives  425 us (65%)
  starting transfers between devices  127 us (19%)
  local copies, waits for them, and re-layouts  39.4 us (6%)
  other arithmetic  22.9 us (3%)
  waiting for transfers between devices  18.6 us (3%)
  between operations  11.2 us (2%)
    psum x4, blocking collectives, global_norm(): return lax.psum(jnp.sum(values * values), ('group', 'lat', 'rad'))  163 us
    psum x3, blocking collectives, per_device(): lax.psum(jnp.sum(direction * mapped), ('group', 'lat', 'rad'))  130 us
    ppermute x23, starting transfers between devices, padded(): lax.ppermute(tail, axis, [(i, (i + 1) % count) for i in range(ends)])  97.1 us
    psum x1, blocking collectives, broadcast(): return lax.psum(kept, axis)  87.5 us
    psum x1, blocking collectives, per_device(): lax.psum(jnp.dot(selector, contrib, precision=lax.Precision.HIGHEST, pref...  40.8 us
    ppermute x23, starting transfers between devices, padded(): lax.ppermute(head, axis, [((i + 1) % count, i) for i in range(ends)])  29.7 us
    concatenate x5, local copies, waits for them, and re-layouts, element_apply(): stacked = jnp.concatenate(pieces, 0)  21.6 us
    ppermute x23, waiting for transfers between devices, padded(): lax.ppermute(tail, axis, [(i, (i + 1) % count) for i in range(ends)])  17.1 us
  transfers between devices with their start and end apart: 46, of which 19 were waited for; matrix products, arithmetic and copies ran while one was open for 4% of the time, Pallas kernels for 0%

commit v1 on v0

--- a/solution.py
+++ b/solution.py
@@ -242,10 +242,16 @@
     )
     selector = (targets == flat_index[None, :]).astype(jnp.float32)
     all_lift = lax.psum(
-        jnp.dot(
-            selector, contrib, precision=lax.Precision.HIGHEST, preferred_element_type=jnp.float32
+        lax.psum(
+            jnp.dot(
+                selector,
+                contrib,
+                precision=lax.Precision.HIGHEST,
+                preferred_element_type=jnp.float32,
+            ),
+            ("lat", "rad"),
         ),
-        ("group", "lat", "rad"),
+        "group",
     )
     own_lift = lax.dynamic_slice_in_dim(
         all_lift, lax.axis_index("lat") * tile_height, tile_height, 0

time: 655 us -> 660 us (level)
    psum x0 -> x1, blocking collectives: none -> 35.3 us  [per_device(): lax.psum(lax.psum(jnp.dot(selector, contrib, precision=lax.Precision.HIGH...]
    psum x1, blocking collectives: 40.8 us -> 11.5 us  [per_device(): lax.psum(jnp.dot(selector, contrib, precision=lax.Precision.HIGHEST, pref...]
where the time goes in v1:
time: 660 us; the launch traced here: 656 us
  blocking collectives  431 us (65%)
  starting transfers between devices  127 us (19%)
  local copies, waits for them, and re-layouts  39.4 us (6%)
  other arithmetic  22.9 us (3%)
  waiting for transfers between devices  18.6 us (3%)
  between operations  11.2 us (2%)
    psum x4, blocking collectives, global_norm(): return lax.psum(jnp.sum(values * values), ('group', 'lat', 'rad'))  163 us
    psum x3, blocking collectives, per_device(): lax.psum(jnp.sum(direction * mapped), ('group', 'lat', 'rad'))  130 us
    ppermute x23, starting transfers between devices, padded(): lax.ppermute(tail, axis, [(i, (i + 1) % count) for i in range(ends)])  97.1 us
    psum x1, blocking collectives, broadcast(): return lax.psum(kept, axis)  87.3 us
    psum x1, blocking collectives, per_device(): lax.psum(lax.psum(jnp.dot(selector, contrib, precision=lax.Precision.HIGH...  35.3 us
    ppermute x23, starting transfers between devices, padded(): lax.ppermute(head, axis, [((i + 1) % count, i) for i in range(ends)])  29.7 us
    concatenate x5, local copies, waits for them, and re-layouts, element_apply(): stacked = jnp.concatenate(pieces, 0)  21.6 us
    ppermute x23, waiting for transfers between devices, padded(): lax.ppermute(tail, axis, [(i, (i + 1) % count) for i in range(ends)])  17.1 us
  transfers between devices with their start and end apart: 46, of which 19 were waited for; matrix products, arithmetic and copies ran while one was open for 4% of the time, Pallas kernels for 0%

profile of v1, /device:TPU:0, one launch (start us, length us, event | category | flops | bytes accessed | tf_op | source)
XLA Modules:
  0.0 656.2 jit_solution(9583999807098391568)
XLA Ops:
  5.3 5.5 collective-permute-start.16
  13.8 4.5 collective-permute-start.3
  21.3 4.5 collective-permute-start
  30.6 4.5 collective-permute-start.4
  40.4 4.5 collective-permute-start.6
  49.7 4.5 collective-permute-start.8
  55.7 4.6 collective-permute-start.18
  63.6 4.5 collective-permute-start.10
  72.9 4.5 collective-permute-start.12
  89.9 7.3 %conditional.13 = (f32[3,2,16,128]{3,0,2,1:T(4,128)S(1)}) conditional(s32[]{:T(128)} %convert_element_type.28, (f32[5,4,18,130]{3,0,2,1:T(8,128)S(1)}, f32[24,24]{1,0:T(8,128)S(1)}, f32[3,17,129]{2,0,1:T(4,128)}, f32[]{:T(128)}) %tuple.375, () %tuple.72), branch_computations={%region_15.16_spmd, %region_16.17_spmd} | conditional | flops 45782880 | bytes 5078236 | solution.py:205
  90.4 4.3 concatenate.158
  98.1 87.3 %psum.77 = bf16[16,256]{1,0:T(8,128)(2,1)S(1)} all-reduce(bf16[16,256]{1,0:T(8,128)(2,1)S(1)} %select_select_fusion), channel_id=1, replica_groups=mesh['group'=8,'lat'=2,'rad'=2] {'group'}, use_global_device_ids=true, to_apply=%region_13.14 | all-reduce | flops 4096 | bytes 16384 | tf_op jit(solution)/shard_map/psum | solution.py:42
  185.4 4.4 all_gather.3
  192.7 4.5 collective-permute-start.22
  200.0 4.5 collective-permute-start.24
  212.8 4.3 concatenate.211
  219.1 40.3 %all-reduce.13 = (f32[]{:T(128)}, f32[]{:T(128)}) all-reduce(f32[]{:T(128)} %get-tuple-element.190, f32[]{:T(128)} %get-tuple-element.189), channel_id=1, replica_groups=mesh['group'=8,'lat'=2,'rad'=2] {'group','lat','rad'}, use_global_device_ids=true, to_apply=%region_18.19 | all-reduce | flops 2 | bytes 16 | tf_op jit(solution)/shard_map/psum | solution.py:222
  261.4 40.9 %psum.80 = f32[]{:T(128)} all-reduce(f32[]{:T(128)} %multiply_reduce_fusion.4), channel_id=1, replica_groups=mesh['group'=8,'lat'=2,'rad'=2] {'group','lat','rad'}, use_global_device_ids=true, to_apply=%region_22.23 | all-reduce | flops 1 | bytes 8 | tf_op jit(solution)/shard_map/psum | solution.py:222
  305.0 5.0 collective-permute-start.28
  312.8 4.5 collective-permute-start.30
  325.6 4.3 concatenate.216
  331.9 43.2 %psum.81 = f32[]{:T(128)} all-reduce(f32[]{:T(128)} %get-tuple-element.399), channel_id=1, replica_groups=mesh['group'=8,'lat'=2,'rad'=2] {'group','lat','rad'}, use_global_device_ids=true, to_apply=%region_24.25 | all-reduce | flops 1 | bytes 8 | tf_op jit(solution)/shard_map/psum | solution.py:230
  377.1 40.4 %psum.82 = f32[]{:T(128)} all-reduce(f32[]{:T(128)} %get-tuple-element.397), channel_id=1, replica_groups=mesh['group'=8,'lat'=2,'rad'=2] {'group','lat','rad'}, use_global_device_ids=true, to_apply=%region_26.27 | all-reduce | flops 1 | bytes 8 | tf_op jit(solution)/shard_map/psum | solution.py:222
  420.2 5.0 collective-permute-start.34
  427.9 4.5 collective-permute-start.36
  447.1 43.4 %psum.83 = f32[]{:T(128)} all-reduce(f32[]{:T(128)} %get-tuple-element.395), channel_id=1, replica_groups=mesh['group'=8,'lat'=2,'rad'=2] {'group','lat','rad'}, use_global_device_ids=true, to_apply=%region_28.29 | all-reduce | flops 1 | bytes 8 | tf_op jit(solution)/shard_map/psum | solution.py:230
  492.5 41.1 %psum.84 = f32[]{:T(128)} all-reduce(f32[]{:T(128)} %multiply_reduce_fusion), channel_id=1, replica_groups=mesh['group'=8,'lat'=2,'rad'=2] {'group','lat','rad'}, use_global_device_ids=true, to_apply=%region_30.31 | all-reduce | flops 1 | bytes 8 | tf_op jit(solution)/shard_map/psum | solution.py:222
  536.3 5.0 collective-permute-start.40
  544.0 4.5 collective-permute-start.42
  563.3 43.2 %psum.85 = f32[]{:T(128)} all-reduce(f32[]{:T(128)} %fusion.707), channel_id=1, replica_groups=mesh['group'=8,'lat'=2,'rad'=2] {'group','lat','rad'}, use_global_device_ids=true, to_apply=%region_32.33 | all-reduce | flops 1 | bytes 8 | tf_op jit(solution)/shard_map/psum | solution.py:230
  608.8 11.5 %psum.86 = f32[64,128]{1,0:T(8,128)S(1)} all-reduce(f32[64,128]{1,0:T(8,128)S(1)} %fusion.711), channel_id=1, replica_groups=mesh['group'=8,'lat'=2,'rad'=2] {'lat','rad'}, use_global_device_ids=true, to_apply=%region_34.35 | all-reduce | flops 8192 | bytes 65536 | tf_op jit(solution)/shard_map/psum | solution.py:245
  620.3 35.3 %psum.87 = f32[64,128]{1,0:T(8,128)S(1)} all-reduce(f32[64,128]{1,0:T(8,128)S(1)} %psum.86), channel_id=1, replica_groups=mesh['group'=8,'lat'=2,'rad'=2] {'group'}, use_global_device_ids=true, to_apply=%region_35.36 | all-reduce | flops 8192 | bytes 65536 | tf_op jit(solution)/shard_map/psum | solution.py:244
  (205 shorter events, 122.4 us)
Async XLA Ops:
  4.0 41.0 %collective-permute-start.17 = (f32[5,2,1,128]{3,0,2,1:T(8,128)S(1)}, f32[5,2,1,128]{3,0,2,1:T(8,128)S(1)}, u32[]{:S(2)}, u32[]{:S(2)}) collective-permute-start(f32[5,2,1,128]{3,0,2,1:T(8,128)S(1)} %get-tuple-element.513), channel_id=1, source_target_pairs={{4,0},{8,4},{12,8},{16,12},{20,16},{24,20},{28,24},{5,1},{9,5},{13... | collective-permute-start | bytes 15368 | tf_op jit(solution)/shard_map/ppermute | solution.py:33
  5.3 39.7 %collective-permute-start.16 = (f32[5,2,1,128]{3,0,2,1:T(8,128)S(1)}, f32[5,2,1,128]{3,0,2,1:T(8,128)S(1)}, u32[]{:S(2)}, u32[]{:S(2)}) collective-permute-start(f32[5,2,1,128]{3,0,2,1:T(8,128)S(1)} %get-tuple-element.512), channel_id=1, source_target_pairs={{0,4},{4,8},{8,12},{12,16},{16,20},{20,24},{24,28},{1,5},{5,9},{9,... | collective-permute-start | bytes 15368 | tf_op jit(solution)/shard_map/ppermute | solution.py:31
  11.8 14.8 %collective-permute-start.1 = (f32[16,1,256]{2,1,0:T(1,128)S(1)}, f32[16,1,256]{2,1,0:T(1,128)S(1)}, u32[]{:S(2)}, u32[]{:S(2)}) collective-permute-start(f32[16,1,256]{2,1,0:T(1,128)S(1)} %get-tuple-element.461), channel_id=1, source_target_pairs={{2,0},{3,1},{6,4},{7,5},{10,8},{11,9},{14,12},{15,13},{18,16},{19,... | collective-permute-start | bytes 49160 | tf_op jit(solution)/shard_map/ppermute | solution.py:33
  13.8 7.4 %collective-permute-start.3 = (f32[1,256]{1,0:T(1,128)S(1)}, f32[1,256]{1,0:T(1,128)S(1)}, u32[]{:S(2)}, u32[]{:S(2)}) collective-permute-start(f32[1,256]{1,0:T(1,128)S(1)} %get-tuple-element.533), channel_id=1, source_target_pairs={{0,2},{1,3},{4,6},{5,7},{8,10},{9,11},{12,14},{13,15},{16,18},{17,... | collective-permute-start | bytes 3080 | tf_op jit(solution)/shard_map/ppermute | solution.py:31
  18.4 7.4 %collective-permute-start.2 = (f32[1,256]{1,0:T(1,128)S(1)}, f32[1,256]{1,0:T(1,128)S(1)}, u32[]{:S(2)}, u32[]{:S(2)}) collective-permute-start(f32[1,256]{1,0:T(1,128)S(1)} %get-tuple-element.532), channel_id=1, source_target_pairs={{2,0},{3,1},{6,4},{7,5},{10,8},{11,9},{14,12},{15,13},{18,16},{19,... | collective-permute-start | bytes 3080 | tf_op jit(solution)/shard_map/ppermute | solution.py:33
  29.3 7.8 %collective-permute-start.5 = (f32[16,1,256]{2,1,0:T(1,128)S(1)}, f32[16,1,256]{2,1,0:T(1,128)S(1)}, u32[]{:S(2)}, u32[]{:S(2)}) collective-permute-start(f32[16,1,256]{2,1,0:T(1,128)S(1)} %get-tuple-element.459), channel_id=1, source_target_pairs={{2,0},{3,1},{6,4},{7,5},{10,8},{11,9},{14,12},{15,13},{18,16},{19,... | collective-permute-start | bytes 49160 | tf_op jit(solution)/shard_map/ppermute | solution.py:33
  30.6 6.5 collective-permute-start.4
  48.4 11.8 %collective-permute-start.9 = (f32[16,1,256]{2,1,0:T(1,128)S(1)}, f32[16,1,256]{2,1,0:T(1,128)S(1)}, u32[]{:S(2)}, u32[]{:S(2)}) collective-permute-start(f32[16,1,256]{2,1,0:T(1,128)S(1)} %get-tuple-element.455), channel_id=1, source_target_pairs={{2,0},{3,1},{6,4},{7,5},{10,8},{11,9},{14,12},{15,13},{18,16},{19,... | collective-permute-start | bytes 49160 | tf_op jit(solution)/shard_map/ppermute | solution.py:33
  49.7 10.5 %collective-permute-start.8 = (f32[16,1,256]{2,1,0:T(1,128)S(1)}, f32[16,1,256]{2,1,0:T(1,128)S(1)}, u32[]{:S(2)}, u32[]{:S(2)}) collective-permute-start(f32[16,1,256]{2,1,0:T(1,128)S(1)} %get-tuple-element.454), channel_id=1, source_target_pairs={{0,2},{1,3},{4,6},{5,7},{8,10},{9,11},{12,14},{13,15},{16,18},{17,... | collective-permute-start | bytes 49160 | tf_op jit(solution)/shard_map/ppermute | solution.py:31
  54.4 13.8 %collective-permute-start.19 = (f32[5,2,18,1]{3,0,2,1:T(8,128)S(1)}, f32[5,2,18,1]{3,0,2,1:T(8,128)S(1)}, u32[]{:S(2)}, u32[]{:S(2)}) collective-permute-start(f32[5,2,18,1]{3,0,2,1:T(8,128)S(1)} %get-tuple-element.511), channel_id=1, source_target_pairs={{2,0},{3,1},{6,4},{7,5},{10,8},{11,9},{14,12},{15,13},{18,16},{19,... | collective-permute-start | bytes 2168 | tf_op jit(solution)/shard_map/ppermute | solution.py:33
  55.7 12.5 %collective-permute-start.18 = (f32[5,2,18,1]{3,0,2,1:T(8,128)S(1)}, f32[5,2,18,1]{3,0,2,1:T(8,128)S(1)}, u32[]{:S(2)}, u32[]{:S(2)}) collective-permute-start(f32[5,2,18,1]{3,0,2,1:T(8,128)S(1)} %get-tuple-element.510), channel_id=1, source_target_pairs={{0,2},{1,3},{4,6},{5,7},{8,10},{9,11},{12,14},{13,15},{16,18},{17,... | collective-permute-start | bytes 2168 | tf_op jit(solution)/shard_map/ppermute | solution.py:31
  62.3 6.2 collective-permute-start.11
  71.6 10.2 %collective-permute-start.13 = (f32[16,1,256]{2,1,0:T(1,128)S(1)}, f32[16,1,256]{2,1,0:T(1,128)S(1)}, u32[]{:S(2)}, u32[]{:S(2)}) collective-permute-start(f32[16,1,256]{2,1,0:T(1,128)S(1)} %get-tuple-element.451), channel_id=1, source_target_pairs={{2,0},{3,1},{6,4},{7,5},{10,8},{11,9},{14,12},{15,13},{18,16},{19,... | collective-permute-start | bytes 49160 | tf_op jit(solution)/shard_map/ppermute | solution.py:33
  72.9 8.9 %collective-permute-start.12 = (f32[16,1,256]{2,1,0:T(1,128)S(1)}, f32[16,1,256]{2,1,0:T(1,128)S(1)}, u32[]{:S(2)}, u32[]{:S(2)}) collective-permute-start(f32[16,1,256]{2,1,0:T(1,128)S(1)} %get-tuple-element.450), channel_id=1, source_target_pairs={{0,2},{1,3},{4,6},{5,7},{8,10},{9,11},{12,14},{13,15},{16,18},{17,... | collective-permute-start | bytes 49160 | tf_op jit(solution)/shard_map/ppermute | solution.py:31
  77.5 11.5 %collective-permute-start.21 = (f32[5,1,18,130]{3,0,2,1:T(8,128)S(1)}, f32[5,1,18,130]{3,0,2,1:T(8,128)S(1)}, u32[]{:S(2)}, u32[]{:S(2)}) collective-permute-start(f32[5,1,18,130]{3,0,2,1:T(8,128)S(1)} %get-tuple-element.449), channel_id=1, source_target_pairs={{1,0},{3,2},{5,4},{7,6},{9,8},{11,10},{13,12},{15,14},{17,16},{19,... | collective-permute-start | bytes 140408 | tf_op jit(solution)/shard_map/ppermute | solution.py:33
  78.8 10.2 %collective-permute-start.20 = (f32[5,1,18,130]{3,0,2,1:T(8,128)S(1)}, f32[5,1,18,130]{3,0,2,1:T(8,128)S(1)}, u32[]{:S(2)}, u32[]{:S(2)}) collective-permute-start(f32[5,1,18,130]{3,0,2,1:T(8,128)S(1)} %get-tuple-element.448), channel_id=1, source_target_pairs={{0,1},{2,3},{4,5},{6,7},{8,9},{10,11},{12,13},{14,15},{16,17},{18,... | collective-permute-start | bytes 140408 | tf_op jit(solution)/shard_map/ppermute | solution.py:31
  85.8 11.4 %collective-permute-start.15 = (f32[1,256]{1,0:T(1,128)}, f32[1,256]{1,0:T(1,128)}, u32[]{:S(2)}, u32[]{:S(2)}) collective-permute-start(f32[1,256]{1,0:T(1,128)} %get-tuple-element.531), channel_id=1, source_target_pairs={{0,2},{1,3},{4,6},{5,7},{8,10},{9,11},{12,14},{13,15},{16,18},{17,... | collective-permute-start | bytes 3080 | tf_op jit(solution)/shard_map/ppermute | solution.py:31
  87.7 9.6 %collective-permute-start.14 = (f32[1,256]{1,0:T(1,128)}, f32[1,256]{1,0:T(1,128)}, u32[]{:S(2)}, u32[]{:S(2)}) collective-permute-start(f32[1,256]{1,0:T(1,128)} %get-tuple-element.530), channel_id=1, source_target_pairs={{2,0},{3,1},{6,4},{7,5},{10,8},{11,9},{14,12},{15,13},{18,16},{19,... | collective-permute-start | bytes 3080 | tf_op jit(solution)/shard_map/ppermute | solution.py:33
  198.7 6.2 collective-permute-start.25
  200.0 6.5 collective-permute-start.24
  303.7 6.3 collective-permute-start.29
  305.0 6.3 collective-permute-start.28
  311.5 6.2 collective-permute-start.31
  312.8 6.5 collective-permute-start.30
  418.9 6.3 collective-permute-start.35
  420.2 6.3 collective-permute-start.34
  426.6 6.2 collective-permute-start.37
  427.9 6.5 collective-permute-start.36
  535.0 6.3 collective-permute-start.41
  536.3 6.3 collective-permute-start.40
  542.7 6.2 collective-permute-start.43
  544.0 6.5 collective-permute-start.42
  (21 other events, 279.1 us)
